TPU v7x, 32 devices: a whole 2x2x4 slice. The times are simulated.
32 devices in a mesh: groups: 2 (over y), date: 8 (over z, x), strip: 2 (over core).
Axes of the slice: x: 2, y: 2, z: 4, core: 2. Of those that a mesh axis runs over, the one named last changes fastest.
Arguments:
- slc_tiles: float32 [2, 16, 32, 1024], P(None, ('groups', 'date'), None, 'strip'), parts along dimension 1, may hold values from -6 to 6
- coreg_shift: int32 [16, 2], P(('groups', 'date')), parts along dimension 0, may hold values from -16 to 16, as said below
- center_freq: float32 [16], P('groups'), parts along dimension 0, may hold values from -0.2 to 0.2
- filter_taps: float32 [17], replicated, may hold values from 0.05 to 0.4
- owner_table: int32 [16], P('groups'), parts along dimension 0, may hold values from 0 to 7, each once
Outputs:
- phases: float32 [2, 16, 8192], P(None, 'groups', ('date', 'strip')), parts along dimension 1
There are 2 independent parts, one for each index of `groups`. A program takes and returns all parts, laid end to end along the dimension named above; an argument that names none is the same for every part. Nothing has to cross between parts.
Inputs may be any that keep to these rules, and one draw needn't show every extreme that they name: `coreg_shift`: both 16 and -16 occur in every draw. `owner_table`: a permutation: every index of date owns exactly one block.
All inputs are finite; a program needn't handle non-finite values.
Results may differ from a plain program's by a relative error of at most 0.0003.
Values sent between devices are 32-bit elements; how exact they have to be, the bound alone decides.
No kernel may reach another device: no remote copies, remote signals or barrier semaphores. Data moves between devices by JAX's collectives and lax.ppermute only.
A program may use at most 64 MiB of HBM per device.

v0:
```python
import math
import jax
import jax.numpy as jnp
from jax import lax
from jax.sharding import PartitionSpec as P

SMAX = 16
TAPS = 17
ROUNDS = 3
MINI = 8
ITERS = 3


def swapped(value, axis, bit):
    mask = 2**bit
    pairs = [(source, source ^ mask) for source in range(lax.axis_size(axis))]
    return lax.ppermute(value, axis, pairs)


def padded_2(value, sides, width):
    for axis, dim in sides:
        peers, length = (lax.axis_size(axis), value.shape[dim])
        up = [(i, (i + 1) % peers) for i in range(peers - 1)]
        down = [(j, i) for i, j in up]
        last = lax.slice_in_dim(value, length - width, length, axis=dim)
        leading = lax.slice_in_dim(value, 0, width, axis=dim)
        before = lax.ppermute(last, axis, up)
        after = lax.ppermute(leading, axis, down)
        value = jnp.concatenate([before, value, after], axis=dim)
    return value


def look_mean(field):
    layout = field.shape
    folded = field.reshape(layout[:-2] + (layout[-2] // 2, 2, layout[-1] // 2, 2))
    return jnp.sum(folded, axis=(-3, -1)) * 0.25


def partner_view(field, stride):
    layout = field.shape
    folded = field.reshape((layout[0] // (2 * stride), 2, stride) + layout[1:])
    return jnp.flip(folded, axis=1).reshape(layout)


def pair_terms(lower_re, lower_im, stride):
    layout = lower_re.shape
    folded_re = lower_re.reshape((layout[0] // stride, stride) + layout[1:])
    folded_im = lower_im.reshape((layout[0] // stride, stride) + layout[1:])
    full_shape = (2 * layout[0],) + layout[1:]
    terms_re = jnp.stack([folded_re, folded_re], axis=1).reshape(full_shape)
    terms_im = jnp.stack([folded_im, -folded_im], axis=1).reshape(full_shape)
    return (terms_re, terms_im)


def link_phase(intensity, pair_list):
    vec_re = jnp.ones_like(intensity)
    vec_im = jnp.zeros_like(intensity)
    layout = intensity.shape
    for sweep_step in range(ITERS):
        next_re = intensity * vec_re
        next_im = intensity * vec_im
        for terms_re, terms_im, stride in pair_list:
            other_re = partner_view(vec_re, stride)
            other_im = partner_view(vec_im, stride)
            next_re = next_re + terms_re * other_re - terms_im * other_im
            next_im = next_im + terms_re * other_im + terms_im * other_re
        energy = (next_re * next_re + next_im * next_im).reshape(
            (layout[0] // MINI, MINI) + layout[1:]
        )
        length = jnp.sqrt(jnp.sum(energy, axis=1, keepdims=True))
        factor = jnp.broadcast_to(1.0 / jnp.maximum(length, 1.0), energy.shape).reshape(layout)
        vec_re = next_re * factor
        vec_im = next_im * factor
    return (vec_re, vec_im)


def link_block(received):
    date_count = received.shape[1]
    item_count = received.shape[2]
    pair_list = []
    for round_bit in range(ROUNDS):
        stride = 1 << round_bit
        fields = received[2 * round_bit : 2 * round_bit + 2].reshape(
            2, date_count // (2 * stride), 2, stride, item_count
        )
        lower_ifg = jnp.moveaxis(fields, 2, 3).reshape(2, date_count // 2, 2, item_count)
        terms_re, terms_im = pair_terms(lower_ifg[0], lower_ifg[1], stride)
        pair_list.append((terms_re, terms_im, stride))
    brightness = jnp.moveaxis(received[2 * ROUNDS : 2 * ROUNDS + 2], 0, 1)
    vec_re, vec_im = link_phase(brightness, pair_list)
    return jnp.stack([vec_re, vec_im])


def band_matrix(filter_taps, rotation, block_len):
    tap_count = filter_taps.shape[0]
    offsets = jnp.arange(tap_count, dtype=jnp.float32) - tap_count // 2
    tap_re = filter_taps * jnp.cos(rotation * offsets)
    tap_im = filter_taps * jnp.sin(rotation * offsets)
    lag_grid = (
        jnp.arange(block_len + tap_count - 1, dtype=jnp.int32)[:, None]
        - jnp.arange(block_len, dtype=jnp.int32)[None, :]
    )
    picked = lag_grid[:, :, None] == jnp.arange(tap_count, dtype=jnp.int32)[None, None, :]
    mat_re = jnp.sum(jnp.where(picked, tap_re, 0.0), axis=-1)
    mat_im = jnp.sum(jnp.where(picked, tap_im, 0.0), axis=-1)
    upper_half = jnp.concatenate([mat_re, mat_im], axis=1)
    lower_half = jnp.concatenate([-mat_im, mat_re], axis=1)
    return jnp.concatenate([upper_half, lower_half], axis=0)


def band_filter(extended, matrix, block_len, tap_reach):
    components, row_count, total_cols = extended.shape
    out_cols = total_cols - 2 * tap_reach
    nblocks = out_cols // block_len
    left_rim = extended[:, :, :out_cols].reshape(components, row_count, nblocks, block_len)[
        ..., :tap_reach
    ]
    middle = extended[:, :, tap_reach : tap_reach + out_cols].reshape(
        components, row_count, nblocks, block_len
    )
    right_rim = extended[:, :, 2 * tap_reach :].reshape(components, row_count, nblocks, block_len)[
        ..., block_len - tap_reach :
    ]
    windows = jnp.concatenate([left_rim, middle, right_rim], axis=-1)
    joined = jnp.concatenate([windows[0], windows[1]], axis=-1).reshape(row_count * nblocks, -1)
    product = jnp.dot(
        joined, matrix, precision=lax.Precision.HIGHEST, preferred_element_type=jnp.float32
    )
    product = product.reshape(row_count, nblocks, 2, block_len)
    return (
        product[:, :, 0].reshape(row_count, out_cols),
        product[:, :, 1].reshape(row_count, out_cols),
    )


def trade(payload, round_bit):
    return swapped(payload, "date", round_bit)


def shards(slc_tiles, coreg_shift, center_freq, filter_taps, owner_table):
    tap_reach = TAPS // 2
    margin = SMAX + tap_reach
    own_tile = slc_tiles[:, 0]
    row_count = own_tile.shape[1]
    strip_cols = own_tile.shape[2]
    block_len = math.gcd(strip_cols, 128)
    date_count = lax.axis_size("date")
    position = lax.axis_index("date")
    padded = padded_2(own_tile, (("strip", 2),), margin)
    line_blocks = coreg_shift.shape[1]
    grouped = padded.reshape(2, line_blocks, row_count // line_blocks, padded.shape[2])

    def shift_block(segment, amount):
        return lax.dynamic_slice_in_dim(segment, SMAX + amount, strip_cols + 2 * tap_reach, axis=2)

    resampled = jax.vmap(shift_block, in_axes=(1, 0), out_axes=1)(grouped, coreg_shift[0])
    resampled = resampled.reshape(2, row_count, strip_cols + 2 * tap_reach)
    centre = resampled[:, :, tap_reach : tap_reach + strip_cols]
    brightness = look_mean(centre[0] * centre[0] + centre[1] * centre[1])
    half_rows = row_count // 2
    pixel_count = half_rows // 2 * (strip_cols // 2)
    block_pixels = pixel_count // date_count
    bright_fields = brightness.reshape(2, date_count, block_pixels)
    date_ids = jnp.arange(date_count, dtype=jnp.int32)
    own_freq = jnp.sum(jnp.where(date_ids == position, center_freq, 0.0))
    inverse = jnp.zeros((date_count,), jnp.int32).at[owner_table].set(date_ids)
    ifg_fields = []
    for round_bit in range(ROUNDS):
        stride = 1 << round_bit
        parity = position // stride % 2
        partner = jnp.bitwise_xor(position, stride)
        partner_freq = jnp.sum(jnp.where(date_ids == partner, center_freq, 0.0))
        rotation = jnp.pi * (partner_freq - own_freq)
        whole_re, whole_im = band_filter(
            resampled, band_matrix(filter_taps, rotation, block_len), block_len, tap_reach
        )
        filtered = jnp.stack([whole_re, whole_im])
        outgoing = lax.dynamic_slice_in_dim(filtered, (1 - parity) * half_rows, half_rows, axis=1)
        kept_half = lax.dynamic_slice_in_dim(filtered, parity * half_rows, half_rows, axis=1)
        arrived = trade(outgoing, round_bit)
        mine_re, mine_im = (kept_half[0], kept_half[1])
        theirs_re, theirs_im = (arrived[0], arrived[1])
        is_lower = parity == 0
        first_re = jnp.where(is_lower, mine_re, theirs_re)
        first_im = jnp.where(is_lower, mine_im, theirs_im)
        second_re = jnp.where(is_lower, theirs_re, mine_re)
        second_im = jnp.where(is_lower, theirs_im, mine_im)
        ifg_re = look_mean(first_re * second_re + first_im * second_im)
        ifg_im = look_mean(first_im * second_re - first_re * second_im)
        round_fields = jnp.stack([ifg_re, ifg_im]).reshape(2, date_count, block_pixels)
        ifg_fields.append(round_fields)
    outgoing_all = jnp.take(jnp.concatenate(ifg_fields + [bright_fields], axis=0), inverse, axis=1)
    linked = link_block(
        lax.all_to_all(outgoing_all, "date", split_axis=1, concat_axis=1, tiled=True)
    )
    return linked.reshape(2, date_count, 2 * block_pixels)


def solution(mesh):
    in_specs = (
        P(None, ("groups", "date"), None, "strip"),
        P(("groups", "date"), None),
        P("groups"),
        P(),
        P("groups"),
    )
    out_specs = P(None, "groups", ("date", "strip"))
    return jax.shard_map(shards, mesh=mesh, in_specs=in_specs, out_specs=out_specs, check_vma=False)
```

profile of v0, /device:TPU:0, one launch (start us, length us, event | category | flops | bytes accessed | tf_op | source)
XLA Modules:
  0.0 62.4 jit_solution(8768502680218335158)
XLA Ops:
  0.0 0.9 %fusion.65 = (f32[2,32,24]{2,1,0:T(8,128)S(1)}, f32[2,32,24]{2,1,0:T(8,128)S(1)}) fusion(f32[2,32,512]{2,1,0:T(8,128)} %bitcast.407), kind=kLoop, calls=%fused_computation.199 | loop fusion | bytes 24576 | tf_op jit(solution)/shard_map/slice | solution.py:25
  0.9 2.4 %collective-permute-start = (f32[2,32,24]{2,1,0:T(8,128)S(1)}, f32[2,32,24]{2,1,0:T(8,128)S(1)}, u32[]{:S(2)}, u32[]{:S(2)}) collective-permute-start(f32[2,32,24]{2,1,0:T(8,128)S(1)} %get-tuple-element.47), channel_id=1, source_target_pairs={{0,1},{2,3},{4,5},{6,7},{8,9},{10,11},{12,13},{14,15},{16,17},{18,... | collective-permute-start | bytes 18440 | tf_op jit(solution)/shard_map/ppermute | solution.py:27
  3.3 1.3 %collective-permute-start.1 = (f32[2,32,24]{2,1,0:T(8,128)S(1)}, f32[2,32,24]{2,1,0:T(8,128)S(1)}, u32[]{:S(2)}, u32[]{:S(2)}) collective-permute-start(f32[2,32,24]{2,1,0:T(8,128)S(1)} %get-tuple-element.48), channel_id=1, source_target_pairs={{1,0},{3,2},{5,4},{7,6},{9,8},{11,10},{13,12},{15,14},{17,16},{19,... | collective-permute-start | bytes 18440 | tf_op jit(solution)/shard_map/ppermute | solution.py:28
  4.6 0.7 %compare_select_fusion.2 = s32[8]{0:T(128)S(1)} fusion(s32[8]{0:T(128)} %param.9), kind=kLoop, calls=%fused_computation.163 | loop fusion | flops 24 | bytes 64 | tf_op jit(solution)/shard_map/select_n | solution.py:166
  5.3 0.6 scatter_custom_fusion
  5.9 1.3 %fusion.45 = (f32[]{:T(128)}, f32[]{:T(128)}, f32[]{:T(128)}, f32[]{:T(128)}) fusion(f32[8]{0:T(128)} %param.7, s32[]{:T(128)S(6)} %xor.11, s32[]{:T(128)S(6)} %axis_index.15, s32[]{:T(128)S(6)} %xor.9, s32[]{:T(128)S(6)} %xor.10), kind=kLoop, calls=%fused_computation.175 | loop fusion | flops 92 | bytes 64 | tf_op jit(solution)/shard_map/reduce_sum | solution.py:172
  11.2 0.7 %or_bitcast_fusion = s32[2]{0:T(128)S(1)} fusion(s32[1,2]{1,0:T(1,128)} %param.6), kind=kLoop, calls=%fused_computation.177 | loop fusion | flops 18 | bytes 16 | tf_op jit(solution)/shard_map/vmap()/gather | solution.py:154
  11.9 0.7 %cosine_multiply_fusion.2 = (f32[17]{0:T(128)S(1)}, f32[17]{0:T(128)S(1)}, f32[17]{0:T(128)S(1)}, f32[17]{0:T(128)S(1)}, f32[17]{0:T(128)S(1)}, /*index=5*/f32[17]{0:T(128)S(1)}) fusion(f32[17]{0:T(128)} %param.8, f32[]{:T(128)S(6)} %mul.430, f32[]{:T(128)S(6)} %mul.445, f32[]{:T(128)S(6)} %mul.460), kind=kLoop, calls=%fused_computation.183 | loop fusion | flops 170 | bytes 488 | tf_op jit(solution)/shard_map/mul | solution.py:97
  12.6 1.0 %select_reduce_fusion = (f32[144,128]{1,0:T(8,128)S(1)}, f32[144,128]{1,0:T(8,128)S(1)}, f32[144,128]{1,0:T(8,128)S(1)}, f32[144,128]{1,0:T(8,128)S(1)}, f32[144,128]{1,0:T(8,128)S(1)}, /*index=5*/f32[144,128]{1,0:T(8,128)S(1)}) fusion(f32[17]{0:T(128)S(1)} %get-tuple-element.68, s32[144,128]{1,0:T(8,128)S(1)} %iota_subtract_fusion, ...), kind=kLoop, calls=%fused_computation.3 | loop fusion | flops 3962880 | bytes 516504 | tf_op jit(solution)/shard_map/reduce_sum | solution.py:105
  14.0 0.8 %copy.94 = f32[2,2,16,560]{2,0,1,3:T(2,128)S(1)} copy(f32[2,2,16,560]{3,2,1,0:T(8,128)S(1)} %pad_maximum_fusion.1) | data formatting | bytes 286720 | tf_op jit(solution)/shard_map/concatenate | solution.py:29
  14.8 2.0 %gather_fusion.1 = f32[2,2,16,528]{2,1,3,0:T(2,128)S(1)} fusion(f32[2,2,16,560]{2,1,0,3:T(2,128)S(1)} %bitcast.403, s32[2]{0:T(128)S(1)} %or_bitcast_fusion), kind=kCustom, calls=%fused_computation.1 | custom fusion | bytes 270368 | tf_op jit(solution)/shard_map/vmap()/gather | solution.py:154
  18.8 3.5 %collective-permute-start.4 = (f32[2,16,512]{2,0,1:T(2,128)S(1)}, f32[2,16,512]{2,0,1:T(2,128)S(1)}, u32[]{:S(2)}, u32[]{:S(2)}) collective-permute-start(f32[2,16,512]{2,0,1:T(2,128)S(1)} %get-tuple-element.36), channel_id=1, source_target_pairs={{0,8},{2,10},{4,12},{6,14},{8,0},{10,2},{12,4},{14,6},{1,9},{3,11}... | collective-permute-start | bytes 196616 | tf_op jit(solution)/shard_map/ppermute | solution.py:17
  22.9 1.6 %collective-permute-start.3 = (f32[2,16,512]{2,0,1:T(2,128)S(1)}, f32[2,16,512]{2,0,1:T(2,128)S(1)}, u32[]{:S(2)}, u32[]{:S(2)}) collective-permute-start(f32[2,16,512]{2,0,1:T(2,128)S(1)} %get-tuple-element.40), channel_id=1, source_target_pairs={{0,4},{2,6},{4,0},{6,2},{8,12},{10,14},{12,8},{14,10},{1,5},{3,7},... | collective-permute-start | bytes 196616 | tf_op jit(solution)/shard_map/ppermute | solution.py:17
  25.2 1.6 %collective-permute-start.2 = (f32[2,16,512]{2,0,1:T(2,128)S(1)}, f32[2,16,512]{2,0,1:T(2,128)S(1)}, u32[]{:S(2)}, u32[]{:S(2)}) collective-permute-start(f32[2,16,512]{2,0,1:T(2,128)S(1)} %get-tuple-element.44), channel_id=1, source_target_pairs={{0,2},{2,0},{4,6},{6,4},{8,10},{10,8},{12,14},{14,12},{1,3},{3,1},... | collective-permute-start | bytes 196616 | tf_op jit(solution)/shard_map/ppermute | solution.py:17
  26.8 5.5 %add.228 = f32[16,2,256,2]{3,2,1,0:T(8,128)} reshape(f32[1,32,512]{2,1,0:T(8,128)S(1)} %fusion.12) | data formatting | bytes 131072 | tf_op jit(solution)/shard_map/add | solution.py:159
  32.3 2.8 %reduce_sum.196 = f32[16,256]{1,0:T(8,128)S(1)} reduce(f32[16,2,256,2]{3,2,1,0:T(8,128)} %add.228, f32[]{:T(128)} %constant.95.clone.1), dimensions={1,3}, to_apply=%region_17.18 | reduce | flops 12288 | bytes 81924 | tf_op jit(solution)/shard_map/reduce_sum | solution.py:36
  35.4 2.1 %add.226 = f32[8,2,256,2]{3,2,1,0:T(8,128)S(1)} reshape(f32[16,512]{1,0:T(8,128)S(1)} %get-tuple-element.6) | data formatting | bytes 65536 | tf_op jit(solution)/shard_map/add | solution.py:188
  37.8 2.1 %sub.173 = f32[8,2,256,2]{3,2,1,0:T(8,128)S(1)} reshape(f32[16,512]{1,0:T(8,128)S(1)} %get-tuple-element.5) | data formatting | bytes 65536 | tf_op jit(solution)/shard_map/sub | solution.py:189
  40.6 2.1 %add.221 = f32[8,2,256,2]{3,2,1,0:T(8,128)S(1)} reshape(f32[16,512]{1,0:T(8,128)S(1)} %get-tuple-element.8) | data formatting | bytes 65536 | tf_op jit(solution)/shard_map/add | solution.py:188
  43.0 2.1 %sub.168 = f32[8,2,256,2]{3,2,1,0:T(8,128)S(1)} reshape(f32[16,512]{1,0:T(8,128)S(1)} %get-tuple-element.7) | data formatting | bytes 65536 | tf_op jit(solution)/shard_map/sub | solution.py:189
  45.8 2.1 %add.216 = f32[8,2,256,2]{3,2,1,0:T(8,128)S(1)} reshape(f32[16,512]{1,0:T(8,128)S(1)} %get-tuple-element.10) | data formatting | bytes 65536 | tf_op jit(solution)/shard_map/add | solution.py:188
  48.3 2.1 %sub.163 = f32[8,2,256,2]{3,2,1,0:T(8,128)S(1)} reshape(f32[16,512]{1,0:T(8,128)S(1)} %get-tuple-element.9) | data formatting | bytes 65536 | tf_op jit(solution)/shard_map/sub | solution.py:189
  51.5 9.3 %all_to_all.5 = f32[8,8,256]{2,0,1:T(8,128)S(1)} all-to-all(f32[8,8,256]{2,0,1:T(8,128)S(1)} %select_bitcast_fusion), channel_id=1, replica_groups=mesh['groups'=2,'date'=8,'strip'=2] {'date'}, dimensions={1} | all-to-all | bytes 131072 | tf_op jit(solution)/shard_map/all_to_all | solution.py:194
  61.8 0.6 pad_maximum_fusion.2
  (115 shorter events, 7.7 us)
Async XLA Ops:
  0.0 13.9 %copy-start = (f32[2,1,32,512]{3,2,1,0:T(8,128)S(1)}, f32[2,1,32,512]{3,2,1,0:T(8,128)}, u32[]{:S(2)}) copy-start(f32[2,1,32,512]{3,2,1,0:T(8,128)} %param.5) | copy-start | bytes 393220
  0.9 13.0 %collective-permute-start = (f32[2,32,24]{2,1,0:T(8,128)S(1)}, f32[2,32,24]{2,1,0:T(8,128)S(1)}, u32[]{:S(2)}, u32[]{:S(2)}) collective-permute-start(f32[2,32,24]{2,1,0:T(8,128)S(1)} %get-tuple-element.47), channel_id=1, source_target_pairs={{0,1},{2,3},{4,5},{6,7},{8,9},{10,11},{12,13},{14,15},{16,17},{18,... | collective-permute-start | bytes 18440 | tf_op jit(solution)/shard_map/ppermute | solution.py:27
  3.3 10.6 %collective-permute-start.1 = (f32[2,32,24]{2,1,0:T(8,128)S(1)}, f32[2,32,24]{2,1,0:T(8,128)S(1)}, u32[]{:S(2)}, u32[]{:S(2)}) collective-permute-start(f32[2,32,24]{2,1,0:T(8,128)S(1)} %get-tuple-element.48), channel_id=1, source_target_pairs={{1,0},{3,2},{5,4},{7,6},{9,8},{11,10},{13,12},{15,14},{17,16},{19,... | collective-permute-start | bytes 18440 | tf_op jit(solution)/shard_map/ppermute | solution.py:28
  18.8 16.4 %collective-permute-start.4 = (f32[2,16,512]{2,0,1:T(2,128)S(1)}, f32[2,16,512]{2,0,1:T(2,128)S(1)}, u32[]{:S(2)}, u32[]{:S(2)}) collective-permute-start(f32[2,16,512]{2,0,1:T(2,128)S(1)} %get-tuple-element.36), channel_id=1, source_target_pairs={{0,8},{2,10},{4,12},{6,14},{8,0},{10,2},{12,4},{14,6},{1,9},{3,11}... | collective-permute-start | bytes 196616 | tf_op jit(solution)/shard_map/ppermute | solution.py:17
  22.9 17.4 %collective-permute-start.3 = (f32[2,16,512]{2,0,1:T(2,128)S(1)}, f32[2,16,512]{2,0,1:T(2,128)S(1)}, u32[]{:S(2)}, u32[]{:S(2)}) collective-permute-start(f32[2,16,512]{2,0,1:T(2,128)S(1)} %get-tuple-element.40), channel_id=1, source_target_pairs={{0,4},{2,6},{4,0},{6,2},{8,12},{10,14},{12,8},{14,10},{1,5},{3,7},... | collective-permute-start | bytes 196616 | tf_op jit(solution)/shard_map/ppermute | solution.py:17
  25.2 20.3 %collective-permute-start.2 = (f32[2,16,512]{2,0,1:T(2,128)S(1)}, f32[2,16,512]{2,0,1:T(2,128)S(1)}, u32[]{:S(2)}, u32[]{:S(2)}) collective-permute-start(f32[2,16,512]{2,0,1:T(2,128)S(1)} %get-tuple-element.44), channel_id=1, source_target_pairs={{0,2},{2,0},{4,6},{6,4},{8,10},{10,8},{12,14},{14,12},{1,3},{3,1},... | collective-permute-start | bytes 196616 | tf_op jit(solution)/shard_map/ppermute | solution.py:17
where the time goes:
time: 62.7 us; the launch traced here: 62.4 us
  local copies, waits for them, and re-layouts  24.4 us (39%)
  other arithmetic  12.2 us (19%)
  starting transfers between devices  10.4 us (17%)
  blocking collectives  9.28 us (15%)
  between operations  4.92 us (8%)
  matrix products  1.25 us (2%)
    all_to_all x1, blocking collectives, shards(): lax.all_to_all(outgoing_all, 'date', split_axis=1, concat_axis=1, tiled=T...  9.28 us
    ppermute x3, starting transfers between devices, swapped(): return lax.ppermute(value, axis, pairs)  6.67 us
    sub x3, local copies, waits for them, and re-layouts, shards(): ifg_im = look_mean(first_im * second_re - first_re * second_im)  6.25 us
    add x3, local copies, waits for them, and re-layouts, shards(): ifg_re = look_mean(first_re * second_re + first_im * second_im)  6.25 us
    add x1, local copies, waits for them, and re-layouts, shards(): brightness = look_mean(centre[0] * centre[0] + centre[1] * centre[1])  5.48 us
    reduce_sum x7, other arithmetic, look_mean(): return jnp.sum(folded, axis=(-3, -1)) * 0.25  4.88 us
    ppermute x1, starting transfers between devices, padded_2(): before = lax.ppermute(last, axis, up)  2.39 us
    gather x1, local copies, waits for them, and re-layouts, shift_block(): lax.dynamic_slice_in_dim(segment, SMAX + amount, strip_cols + 2 * tap_rea...  2.01 us
  transfers between devices with their start and end apart: 5, of which 0 were waited for; matrix products, arithmetic and copies ran while one was open for 40% of the time, Pallas kernels for 0%

commit v1 on v0

--- a/solution.py
+++ b/solution.py
@@ -191,7 +191,12 @@
         ifg_fields.append(round_fields)
     outgoing_all = jnp.take(jnp.concatenate(ifg_fields + [bright_fields], axis=0), inverse, axis=1)
     linked = link_block(
-        lax.all_to_all(outgoing_all, "date", split_axis=1, concat_axis=1, tiled=True)
+        jnp.concatenate(
+            lax.all_to_all(
+                jnp.stack(jnp.split(outgoing_all, lax.axis_size("date"), axis=1)), "date", 0, 0
+            ),
+            axis=1,
+        )
     )
     return linked.reshape(2, date_count, 2 * block_pixels)
 

time: 62.7 us -> 62.8 us (level)
  no operation moved by 1% of the time
where the time goes in v1:
time: 62.8 us; the launch traced here: 62.5 us
  local copies, waits for them, and re-layouts  24.4 us (39%)
  other arithmetic  12.2 us (19%)
  starting transfers between devices  10.4 us (17%)
  blocking collectives  9.29 us (15%)
  between operations  4.98 us (8%)
  matrix products  1.25 us (2%)
    all_to_all x1, blocking collectives, shards(): lax.all_to_all(jnp.stack(jnp.split(outgoing_all, lax.axis_size('date'), a...  9.29 us
    ppermute x3, starting transfers between devices, swapped(): return lax.ppermute(value, axis, pairs)  6.67 us
    sub x3, local copies, waits for them, and re-layouts, shards(): ifg_im = look_mean(first_im * second_re - first_re * second_im)  6.25 us
    add x3, local copies, waits for them, and re-layouts, shards(): ifg_re = look_mean(first_re * second_re + first_im * second_im)  6.25 us
    add x1, local copies, waits for them, and re-layouts, shards(): brightness = look_mean(centre[0] * centre[0] + centre[1] * centre[1])  5.48 us
    reduce_sum x7, other arithmetic, look_mean(): return jnp.sum(folded, axis=(-3, -1)) * 0.25  4.88 us
    ppermute x1, starting transfers between devices, padded_2(): before = lax.ppermute(last, axis, up)  2.39 us
    gather x1, local copies, waits for them, and re-layouts, shift_block(): lax.dynamic_slice_in_dim(segment, SMAX + amount, strip_cols + 2 * tap_rea...  2.01 us
  transfers between devices with their start and end apart: 5, of which 0 were waited for; matrix products, arithmetic and copies ran while one was open for 40% of the time, Pallas kernels for 0%

profile of v1, /device:TPU:0, one launch (start us, length us, event | category | flops | bytes accessed | tf_op | source)
XLA Modules:
  0.0 62.5 jit_solution(18054526010144742305)
XLA Ops:
  0.0 0.9 %fusion.65 = (f32[2,32,24]{2,1,0:T(8,128)S(1)}, f32[2,32,24]{2,1,0:T(8,128)S(1)}) fusion(f32[2,32,512]{2,1,0:T(8,128)} %bitcast.447), kind=kLoop, calls=%fused_computation.215 | loop fusion | bytes 24576 | tf_op jit(solution)/shard_map/slice | solution.py:25
  0.9 2.4 %collective-permute-start = (f32[2,32,24]{2,1,0:T(8,128)S(1)}, f32[2,32,24]{2,1,0:T(8,128)S(1)}, u32[]{:S(2)}, u32[]{:S(2)}) collective-permute-start(f32[2,32,24]{2,1,0:T(8,128)S(1)} %get-tuple-element.47), channel_id=1, source_target_pairs={{0,1},{2,3},{4,5},{6,7},{8,9},{10,11},{12,13},{14,15},{16,17},{18,... | collective-permute-start | bytes 18440 | tf_op jit(solution)/shard_map/ppermute | solution.py:27
  3.3 1.3 %collective-permute-start.1 = (f32[2,32,24]{2,1,0:T(8,128)S(1)}, f32[2,32,24]{2,1,0:T(8,128)S(1)}, u32[]{:S(2)}, u32[]{:S(2)}) collective-permute-start(f32[2,32,24]{2,1,0:T(8,128)S(1)} %get-tuple-element.48), channel_id=1, source_target_pairs={{1,0},{3,2},{5,4},{7,6},{9,8},{11,10},{13,12},{15,14},{17,16},{19,... | collective-permute-start | bytes 18440 | tf_op jit(solution)/shard_map/ppermute | solution.py:28
  4.6 0.7 %compare_select_fusion.2 = s32[8]{0:T(128)S(1)} fusion(s32[8]{0:T(128)} %param.9), kind=kLoop, calls=%fused_computation.179 | loop fusion | flops 24 | bytes 64 | tf_op jit(solution)/shard_map/select_n | solution.py:166
  5.3 0.6 scatter_custom_fusion
  5.9 1.3 %fusion.45 = (f32[]{:T(128)}, f32[]{:T(128)}, f32[]{:T(128)}, f32[]{:T(128)}) fusion(f32[8]{0:T(128)} %param.7, s32[]{:T(128)S(6)} %xor.11, s32[]{:T(128)S(6)} %axis_index.15, s32[]{:T(128)S(6)} %xor.9, s32[]{:T(128)S(6)} %xor.10), kind=kLoop, calls=%fused_computation.191 | loop fusion | flops 92 | bytes 64 | tf_op jit(solution)/shard_map/reduce_sum | solution.py:172
  11.2 0.7 %or_bitcast_fusion = s32[2]{0:T(128)S(1)} fusion(s32[1,2]{1,0:T(1,128)} %param.6), kind=kLoop, calls=%fused_computation.193 | loop fusion | flops 18 | bytes 16 | tf_op jit(solution)/shard_map/vmap()/gather | solution.py:154
  11.9 0.7 %cosine_multiply_fusion.2 = (f32[17]{0:T(128)S(1)}, f32[17]{0:T(128)S(1)}, f32[17]{0:T(128)S(1)}, f32[17]{0:T(128)S(1)}, f32[17]{0:T(128)S(1)}, /*index=5*/f32[17]{0:T(128)S(1)}) fusion(f32[17]{0:T(128)} %param.8, f32[]{:T(128)S(6)} %mul.430, f32[]{:T(128)S(6)} %mul.445, f32[]{:T(128)S(6)} %mul.460), kind=kLoop, calls=%fused_computation.199 | loop fusion | flops 170 | bytes 488 | tf_op jit(solution)/shard_map/mul | solution.py:97
  12.6 1.0 %select_reduce_fusion = (f32[144,128]{1,0:T(8,128)S(1)}, f32[144,128]{1,0:T(8,128)S(1)}, f32[144,128]{1,0:T(8,128)S(1)}, f32[144,128]{1,0:T(8,128)S(1)}, f32[144,128]{1,0:T(8,128)S(1)}, /*index=5*/f32[144,128]{1,0:T(8,128)S(1)}) fusion(f32[17]{0:T(128)S(1)} %get-tuple-element.68, s32[144,128]{1,0:T(8,128)S(1)} %iota_subtract_fusion, ...), kind=kLoop, calls=%fused_computation.3 | loop fusion | flops 3962880 | bytes 516504 | tf_op jit(solution)/shard_map/reduce_sum | solution.py:105
  14.0 0.8 %copy.101 = f32[2,2,16,560]{2,0,1,3:T(2,128)S(1)} copy(f32[2,2,16,560]{3,2,1,0:T(8,128)S(1)} %pad_maximum_fusion.1) | data formatting | bytes 286720 | tf_op jit(solution)/shard_map/concatenate | solution.py:29
  14.8 2.0 %gather_fusion.1 = f32[2,2,16,528]{2,1,3,0:T(2,128)S(1)} fusion(f32[2,2,16,560]{2,1,0,3:T(2,128)S(1)} %bitcast.438, s32[2]{0:T(128)S(1)} %or_bitcast_fusion), kind=kCustom, calls=%fused_computation.1 | custom fusion | bytes 270368 | tf_op jit(solution)/shard_map/vmap()/gather | solution.py:154
  18.8 3.5 %collective-permute-start.4 = (f32[2,16,512]{2,0,1:T(2,128)S(1)}, f32[2,16,512]{2,0,1:T(2,128)S(1)}, u32[]{:S(2)}, u32[]{:S(2)}) collective-permute-start(f32[2,16,512]{2,0,1:T(2,128)S(1)} %get-tuple-element.36), channel_id=1, source_target_pairs={{0,8},{2,10},{4,12},{6,14},{8,0},{10,2},{12,4},{14,6},{1,9},{3,11}... | collective-permute-start | bytes 196616 | tf_op jit(solution)/shard_map/ppermute | solution.py:17
  22.9 1.6 %collective-permute-start.3 = (f32[2,16,512]{2,0,1:T(2,128)S(1)}, f32[2,16,512]{2,0,1:T(2,128)S(1)}, u32[]{:S(2)}, u32[]{:S(2)}) collective-permute-start(f32[2,16,512]{2,0,1:T(2,128)S(1)} %get-tuple-element.40), channel_id=1, source_target_pairs={{0,4},{2,6},{4,0},{6,2},{8,12},{10,14},{12,8},{14,10},{1,5},{3,7},... | collective-permute-start | bytes 196616 | tf_op jit(solution)/shard_map/ppermute | solution.py:17
  25.2 1.6 %collective-permute-start.2 = (f32[2,16,512]{2,0,1:T(2,128)S(1)}, f32[2,16,512]{2,0,1:T(2,128)S(1)}, u32[]{:S(2)}, u32[]{:S(2)}) collective-permute-start(f32[2,16,512]{2,0,1:T(2,128)S(1)} %get-tuple-element.44), channel_id=1, source_target_pairs={{0,2},{2,0},{4,6},{6,4},{8,10},{10,8},{12,14},{14,12},{1,3},{3,1},... | collective-permute-start | bytes 196616 | tf_op jit(solution)/shard_map/ppermute | solution.py:17
  26.8 5.5 %add.228 = f32[16,2,256,2]{3,2,1,0:T(8,128)} reshape(f32[1,32,512]{2,1,0:T(8,128)S(1)} %fusion.12) | data formatting | bytes 131072 | tf_op jit(solution)/shard_map/add | solution.py:159
  32.3 2.8 %reduce_sum.196 = f32[16,256]{1,0:T(8,128)S(1)} reduce(f32[16,2,256,2]{3,2,1,0:T(8,128)} %add.228, f32[]{:T(128)} %constant.95.clone.1), dimensions={1,3}, to_apply=%region_17.18 | reduce | flops 12288 | bytes 81924 | tf_op jit(solution)/shard_map/reduce_sum | solution.py:36
  35.4 2.1 %add.226 = f32[8,2,256,2]{3,2,1,0:T(8,128)S(1)} reshape(f32[16,512]{1,0:T(8,128)S(1)} %get-tuple-element.6) | data formatting | bytes 65536 | tf_op jit(solution)/shard_map/add | solution.py:188
  37.8 2.1 %sub.173 = f32[8,2,256,2]{3,2,1,0:T(8,128)S(1)} reshape(f32[16,512]{1,0:T(8,128)S(1)} %get-tuple-element.5) | data formatting | bytes 65536 | tf_op jit(solution)/shard_map/sub | solution.py:189
  40.6 2.1 %add.221 = f32[8,2,256,2]{3,2,1,0:T(8,128)S(1)} reshape(f32[16,512]{1,0:T(8,128)S(1)} %get-tuple-element.8) | data formatting | bytes 65536 | tf_op jit(solution)/shard_map/add | solution.py:188
  43.0 2.1 %sub.168 = f32[8,2,256,2]{3,2,1,0:T(8,128)S(1)} reshape(f32[16,512]{1,0:T(8,128)S(1)} %get-tuple-element.7) | data formatting | bytes 65536 | tf_op jit(solution)/shard_map/sub | solution.py:189
  45.8 2.1 %add.216 = f32[8,2,256,2]{3,2,1,0:T(8,128)S(1)} reshape(f32[16,512]{1,0:T(8,128)S(1)} %get-tuple-element.10) | data formatting | bytes 65536 | tf_op jit(solution)/shard_map/add | solution.py:188
  48.3 2.1 %sub.163 = f32[8,2,256,2]{3,2,1,0:T(8,128)S(1)} reshape(f32[16,512]{1,0:T(8,128)S(1)} %get-tuple-element.9) | data formatting | bytes 65536 | tf_op jit(solution)/shard_map/sub | solution.py:189
  51.6 9.3 %all_to_all.5 = f32[8,8,1,256]{3,1,2,0:T(8,128)S(1)} all-to-all(f32[8,8,1,256]{3,1,2,0:T(8,128)S(1)} %constant_dynamic-update-slice_fusion), channel_id=1, replica_groups=mesh['groups'=2,'date'=8,'strip'=2] {'date'}, dimensions={0} | all-to-all | bytes 131072 | tf_op jit(solution)/shard_map/all_to_all | solution.py:195
  61.9 0.6 pad_maximum_fusion.2
  (123 shorter events, 7.8 us)
Async XLA Ops:
  0.0 13.9 %copy-start = (f32[2,1,32,512]{3,2,1,0:T(8,128)S(1)}, f32[2,1,32,512]{3,2,1,0:T(8,128)}, u32[]{:S(2)}) copy-start(f32[2,1,32,512]{3,2,1,0:T(8,128)} %param.5) | copy-start | bytes 393220
  0.9 13.0 %collective-permute-start = (f32[2,32,24]{2,1,0:T(8,128)S(1)}, f32[2,32,24]{2,1,0:T(8,128)S(1)}, u32[]{:S(2)}, u32[]{:S(2)}) collective-permute-start(f32[2,32,24]{2,1,0:T(8,128)S(1)} %get-tuple-element.47), channel_id=1, source_target_pairs={{0,1},{2,3},{4,5},{6,7},{8,9},{10,11},{12,13},{14,15},{16,17},{18,... | collective-permute-start | bytes 18440 | tf_op jit(solution)/shard_map/ppermute | solution.py:27
  3.3 10.6 %collective-permute-start.1 = (f32[2,32,24]{2,1,0:T(8,128)S(1)}, f32[2,32,24]{2,1,0:T(8,128)S(1)}, u32[]{:S(2)}, u32[]{:S(2)}) collective-permute-start(f32[2,32,24]{2,1,0:T(8,128)S(1)} %get-tuple-element.48), channel_id=1, source_target_pairs={{1,0},{3,2},{5,4},{7,6},{9,8},{11,10},{13,12},{15,14},{17,16},{19,... | collective-permute-start | bytes 18440 | tf_op jit(solution)/shard_map/ppermute | solution.py:28
  18.8 16.4 %collective-permute-start.4 = (f32[2,16,512]{2,0,1:T(2,128)S(1)}, f32[2,16,512]{2,0,1:T(2,128)S(1)}, u32[]{:S(2)}, u32[]{:S(2)}) collective-permute-start(f32[2,16,512]{2,0,1:T(2,128)S(1)} %get-tuple-element.36), channel_id=1, source_target_pairs={{0,8},{2,10},{4,12},{6,14},{8,0},{10,2},{12,4},{14,6},{1,9},{3,11}... | collective-permute-start | bytes 196616 | tf_op jit(solution)/shard_map/ppermute | solution.py:17
  22.9 17.4 %collective-permute-start.3 = (f32[2,16,512]{2,0,1:T(2,128)S(1)}, f32[2,16,512]{2,0,1:T(2,128)S(1)}, u32[]{:S(2)}, u32[]{:S(2)}) collective-permute-start(f32[2,16,512]{2,0,1:T(2,128)S(1)} %get-tuple-element.40), channel_id=1, source_target_pairs={{0,4},{2,6},{4,0},{6,2},{8,12},{10,14},{12,8},{14,10},{1,5},{3,7},... | collective-permute-start | bytes 196616 | tf_op jit(solution)/shard_map/ppermute | solution.py:17
  25.2 20.3 %collective-permute-start.2 = (f32[2,16,512]{2,0,1:T(2,128)S(1)}, f32[2,16,512]{2,0,1:T(2,128)S(1)}, u32[]{:S(2)}, u32[]{:S(2)}) collective-permute-start(f32[2,16,512]{2,0,1:T(2,128)S(1)} %get-tuple-element.44), channel_id=1, source_target_pairs={{0,2},{2,0},{4,6},{6,4},{8,10},{10,8},{12,14},{14,12},{1,3},{3,1},... | collective-permute-start | bytes 196616 | tf_op jit(solution)/shard_map/ppermute | solution.py:17
